TPU v7x, 512 devices: a whole 4x4x16 slice. The times are simulated.
512 devices in a mesh: dp: 16 (over z), fsdp: 32 (over x, y, core).
Axes of the slice: x: 4, y: 4, z: 16, core: 2. Of those that a mesh axis runs over, the one named last changes fastest.
Arguments:
- txt_tokens: bfloat16 [512, 8, 3072], P(('dp', 'fsdp')), may hold values from -6 to 6
- concept_table: bfloat16 [4096, 3072], P('dp'), may hold values from -6 to 6
- concept_ids: int32 [512], P(('dp', 'fsdp')), may hold values from 0 to 4095
- positions: int32 [512], P(('dp', 'fsdp')), may hold values from 0 to 7
- timesteps: int32 [512], P(('dp', 'fsdp')), may hold values from 0 to 63
- counts: int32 [4096], P('dp'), may hold values from 1 to 16
- mod_table: bfloat16 [64, 2, 3072], P(None, None, 'fsdp'), may hold values from -1.5 to 1.5
- kv_weight: bfloat16 [3072, 3072], P('fsdp'), may hold values from -0.109375 to 0.109375
- kv_bias: float32 [3072], replicated, may hold values from -3 to 3
- key_gain: float32 [128], replicated, may hold values from 0.5 to 1.5
- img_query: bfloat16 [512, 192, 1536], P(('dp', 'fsdp')), may hold values from -256 to 256
- img_key: bfloat16 [512, 192, 1536], P(('dp', 'fsdp')), may hold values from -6 to 6
- img_value: bfloat16 [512, 192, 1536], P(('dp', 'fsdp')), may hold values from -6 to 6
- out_grad: bfloat16 [512, 192, 1536], P(('dp', 'fsdp')), may hold values from -6 to 6
Outputs:
- table_grad: float32 [4096, 3072], P('dp', 'fsdp')
Inputs may be any that keep to these rules, and one draw needn't show every extreme that they name: `concept_ids`: concept of each sample, some concepts far more common than others.
All inputs are finite; a program needn't handle non-finite values.
Results may differ from a plain program's by a relative error of at most 0.0083.
Values may be sent and summed in bfloat16 or wider, within the bound.
A program may use at most 64 MiB of HBM per device.

v0:
```python
import jax
import jax.numpy as jnp
from jax import lax
from jax.sharding import PartitionSpec as P

EPSILON = 1e-06


def layer_norm(values):
    centre = jnp.mean(values, -1, keepdims=True)
    spread = jnp.mean((values - centre) ** 2, -1, keepdims=True)
    inverse = lax.rsqrt(spread + EPSILON)
    return ((values - centre) * inverse, inverse[..., 0])


def shards(
    txt_tokens,
    concept_table,
    concept_ids,
    positions,
    timesteps,
    counts,
    mod_table,
    kv_weight,
    kv_bias,
    key_gain,
    img_query,
    img_key,
    img_value,
    out_grad,
):
    highest = lax.Precision.HIGHEST
    fsdp_size = lax.axis_size("fsdp")
    column = lax.axis_index("fsdp")
    tok_len = txt_tokens.shape[1]
    model_width = txt_tokens.shape[2]
    slice_width = kv_weight.shape[0]
    kv_width = kv_weight.shape[1]
    head_width = kv_width // 2
    head_dim = key_gain.shape[0]
    head_count = head_width // head_dim
    img_len = img_query.shape[1]
    bucket_count = mod_table.shape[0]
    root_dh = jnp.sqrt(jnp.float32(head_dim))
    table_hat, table_rstd = layer_norm(concept_table.astype(jnp.float32))
    table_part = lax.dynamic_slice_in_dim(
        table_hat.astype(jnp.bfloat16), column * slice_width, slice_width, 1
    )
    table_all = lax.all_gather(table_part, "dp", axis=0, tiled=True)
    own_hat = layer_norm(txt_tokens[0].astype(jnp.float32))[0].astype(jnp.bfloat16)
    labels = jnp.stack([concept_ids[0], positions[0], timesteps[0]])
    label_tile = jnp.tile(labels[None, :], (1, fsdp_size))
    token_cols, label_cols = (
        lax.all_to_all(own_hat, "fsdp", split_axis=1, concat_axis=0, tiled=True),
        lax.all_to_all(label_tile, "fsdp", split_axis=1, concat_axis=0, tiled=True),
    )
    group_ids = label_cols[:, 0]
    group_pos = label_cols[:, 1]
    group_time = label_cols[:, 2]
    concept_cols = jnp.take(table_all, group_ids, axis=0)
    token_cols = token_cols.reshape(fsdp_size, tok_len, slice_width)
    is_place = jnp.arange(tok_len, dtype=jnp.int32)[None, :] == group_pos[:, None]
    token_cols = jnp.where(is_place[:, :, None], concept_cols[:, None, :], token_cols)
    pick_time = (jnp.arange(bucket_count, dtype=jnp.int32)[None, :] == group_time[:, None]).astype(
        jnp.bfloat16
    )
    modulation = jnp.dot(
        pick_time,
        mod_table.reshape(bucket_count, 2 * slice_width),
        preferred_element_type=jnp.float32,
    )
    modulation = modulation.reshape(fsdp_size, 2, slice_width)
    shift_cols = modulation[:, 0]
    scale_cols = 1.0 + modulation[:, 1]
    modulated = (
        scale_cols[:, None, :] * token_cols.astype(jnp.float32) + shift_cols[:, None, :]
    ).astype(jnp.bfloat16)
    kv_terms = jnp.dot(
        modulated.reshape(fsdp_size * tok_len, slice_width),
        kv_weight,
        preferred_element_type=jnp.float32,
    )
    kv_terms = kv_terms.reshape(fsdp_size, tok_len, kv_width)
    weight_f = kv_weight.astype(jnp.float32)
    concept_f = concept_cols.astype(jnp.float32)
    side_rows = jnp.stack([scale_cols, scale_cols * concept_f], 1).reshape(
        fsdp_size * 2, slice_width
    )
    side_terms = jnp.dot(side_rows, weight_f, precision=highest).reshape(fsdp_size, 2, kv_width)
    all_terms = jnp.concatenate([kv_terms, side_terms], 1)
    row_block = all_terms.shape[1]
    all_terms = all_terms.reshape(fsdp_size * row_block, kv_width)
    own_rows = lax.psum_scatter(all_terms, "fsdp", scatter_dimension=0, tiled=True)
    kv_rows = own_rows[:tok_len] + kv_bias
    pos_pick = (jnp.arange(tok_len, dtype=jnp.int32) == positions[0]).astype(jnp.float32)
    key_raw = kv_rows[:, :head_width].reshape(tok_len, head_count, head_dim)
    key_inv = lax.rsqrt(jnp.mean(key_raw * key_raw, -1) + EPSILON)
    key_norm = (
        (key_raw * key_inv[..., None] * key_gain).astype(jnp.bfloat16).reshape(tok_len, head_width)
    )
    val_txt = kv_rows[:, head_width:].astype(jnp.bfloat16)
    keys_all = jnp.concatenate([key_norm, img_key[0]], 0).reshape(
        tok_len + img_len, head_count, head_dim
    )
    vals_all = jnp.concatenate([val_txt, img_value[0]], 0).reshape(
        tok_len + img_len, head_count, head_dim
    )
    queries = img_query[0].reshape(img_len, head_count, head_dim)
    scores = (
        jnp.einsum("qhd,khd->hqk", queries, keys_all, preferred_element_type=jnp.float32) / root_dh
    )
    row_top = jnp.max(scores, -1, keepdims=True)
    raised = jnp.exp(scores - row_top)
    prob_full = raised / jnp.sum(raised, -1, keepdims=True)
    prob_low = prob_full.astype(jnp.bfloat16)
    attended = jnp.einsum("hqk,khd->qhd", prob_low, vals_all, preferred_element_type=jnp.float32)
    grad_f = out_grad[0].reshape(img_len, head_count, head_dim).astype(jnp.float32)
    row_delta = jnp.einsum("qhd,qhd->hq", grad_f, attended)
    prob_pos = jnp.einsum("hqk,k->hq", prob_full[:, :, :tok_len], pos_pick, precision=highest)
    val_local = val_txt.reshape(tok_len, head_count, head_dim).astype(jnp.float32)
    val_pos = jnp.einsum("k,khd->hd", pos_pick, val_local, precision=highest)
    grad_prob = jnp.einsum("qhd,hd->hq", grad_f, val_pos, precision=highest)
    grad_score = prob_pos * (grad_prob - row_delta)
    grad_val = jnp.einsum("hq,qhd->hd", prob_pos, grad_f, precision=highest)
    grad_key = (
        jnp.einsum("hq,qhd->hd", grad_score, queries.astype(jnp.float32), precision=highest)
        / root_dh
    )
    raw_pos = jnp.einsum("k,khd->hd", pos_pick, key_raw, precision=highest)
    inv_pos = jnp.einsum("k,kh->h", pos_pick, key_inv, precision=highest)
    normed_key = raw_pos * inv_pos[:, None]
    grad_norm = grad_key * key_gain
    grad_raw = inv_pos[:, None] * (
        grad_norm - normed_key * jnp.mean(grad_norm * normed_key, -1, keepdims=True)
    )
    grad_kv = jnp.concatenate([grad_raw.reshape(head_width), grad_val.reshape(head_width)])[None, :]
    side_mean = (
        jnp.stack(
            [
                jnp.dot(grad_kv[0], own_rows[tok_len], precision=highest),
                jnp.dot(grad_kv[0], own_rows[tok_len + 1], precision=highest),
            ]
        )
        / model_width
    )
    grads_all, sides_all = (
        lax.all_gather(grad_kv, "fsdp", axis=0, tiled=True),
        lax.all_gather(side_mean[None, :], "fsdp", axis=0, tiled=True),
    )
    grad_cols = jnp.dot(grads_all, weight_f.T, precision=highest) * scale_cols
    row_grad = grad_cols - sides_all[:, 0:1] - concept_f * sides_all[:, 1:2]
    owner_scale = table_rstd / counts.astype(jnp.float32)
    conc_total = table_all.shape[0]
    one_hot = (jnp.arange(conc_total, dtype=jnp.int32)[:, None] == group_ids[None, :]).astype(
        jnp.float32
    )
    dense_rows = jnp.dot(one_hot, row_grad, precision=highest)
    owned_rows = lax.psum_scatter(dense_rows, "dp", scatter_dimension=0, tiled=True)
    return owned_rows * owner_scale[:, None]


def solution(mesh):
    placed = (
        P(("dp", "fsdp"), None, None),
        P("dp", None),
        P(("dp", "fsdp")),
        P(("dp", "fsdp")),
        P(("dp", "fsdp")),
        P("dp"),
        P(None, None, "fsdp"),
        P("fsdp", None),
        P(),
        P(),
        P(("dp", "fsdp"), None, None),
        P(("dp", "fsdp"), None, None),
        P(("dp", "fsdp"), None, None),
        P(("dp", "fsdp"), None, None),
    )
    return jax.shard_map(
        shards, mesh=mesh, in_specs=placed, out_specs=P("dp", "fsdp"), check_vma=False
    )
```

profile of v0, /device:TPU:2, one launch (start us, length us, event | category | flops | bytes accessed | tf_op | source)
XLA Modules:
  0.0 369.3 jit_solution(15416597220606547347)
XLA Ops:
  8.7 0.6 tile.2
  9.3 9.3 %all-to-all-start = ((s32[1,32,3]{2,0,1:T(1,128)}), s32[1,32,3]{2,0,1:T(1,128)S(1)}, u32[]{:S(2)}, u32[]{:S(2)}) async-start(s32[1,32,3]{2,0,1:T(1,128)} %tile.2), calls=%async_computation | async-start | bytes 32768 | tf_op jit(solution)/shard_map/all_to_all | solution.py:55
  18.6 0.9 convert_reduce_fusion.1
  19.6 0.9 reshape.234
  20.5 1.7 convert_reduce_fusion
  22.3 2.1 multiply_reduce_fusion
  24.4 0.6 convert_divide_fusion
  25.0 1.1 fusion.32
  26.1 39.8 %all_gather.9 = bf16[4096,96]{1,0:T(8,128)(2,1)S(1)} all-gather(bf16[256,96]{1,0:T(8,128)(2,1)S(1)} %fusion.32), channel_id=1, replica_groups=mesh['dp'=16,'fsdp'=32] {'dp'}, dimensions={0}, use_global_device_ids=true | all-gather | bytes 835584 | tf_op jit(solution)/shard_map/all_gather | solution.py:49
  66.2 0.7 fusion.34
  67.1 7.4 %all-to-all-start.1 = ((bf16[8,32,96]{2,0,1:T(8,128)(2,1)}), bf16[8,32,96]{2,0,1:T(8,128)(2,1)S(1)}, u32[]{:S(2)}, u32[]{:S(2)}) async-start(bf16[8,32,96]{2,0,1:T(8,128)(2,1)} %fusion.34), calls=%async_computation.1 | async-start | bytes 131072 | tf_op jit(solution)/shard_map/all_to_all | solution.py:54
  74.6 0.6 slice_bitcast_fusion.5
  75.2 0.6 gather_fusion
  76.2 0.5 copy-done.11
  76.6 0.5 fusion.19
  77.2 0.6 copy.38
  77.8 3.0 all-to-all-done.1
  80.8 0.6 fusion.21
  81.4 3.4 pad_maximum_fusion
  84.8 5.3 %reshape.229 = f32[320,3072]{1,0:T(8,128)} reshape(f32[32,10,3072]{2,1,0:T(8,128)} %pad_maximum_fusion) | data formatting | bytes 7864320 | tf_op jit(solution)/shard_map/reshape | solution.py:92
  90.2 1.0 copy-done.7
  91.2 0.4 reshape_squeeze.6
  91.6 0.4 concatenate.29
  92.2 0.4 concatenate.31
  92.8 2.2 reshape_squeeze.7
  95.0 1.3 dynamic-slice
  97.0 0.5 broadcast_multiply_fusion.3
  97.4 126.6 %all-reduce.3.cloned.1.call-done = f32[320,3072]{1,0:T(8,128)} async-done(((f32[320,3072]{1,0:T(8,128)}), f32[320,3072]{1,0:T(8,128)}) %all-reduce.3.cloned.1.call-update) | async-done | bytes 3932176
  224.0 0.9 dynamic-slice_add_fusion
  225.2 0.5 fusion.12
  225.7 2.5 fusion.79
  228.2 0.4 broadcast_divide_fusion
  228.6 0.5 convolution_bitcast_fusion
  229.1 0.6 copy-done.2
  229.8 0.9 multiply_reduce_fusion.1
  230.7 1.0 fusion.6
  231.9 2.1 fusion.26
  234.0 1.7 fusion.28
  236.3 0.6 fusion.24
  236.9 1.0 constant_dynamic-slice_fusion.1
  237.9 0.7 multiply_reduce_fusion.3
  238.6 1.4 fusion.68
  240.0 20.8 %all-gather.1 = f32[32,1,2]{2,1,0:T(1,128)S(1)} all-gather(f32[1,1,2]{2,1,0:T(1,128)S(1)} %fusion.68), channel_id=1, replica_groups=mesh['dp'=16,'fsdp'=32] {'fsdp'}, dimensions={0}, use_global_device_ids=true | all-gather | bytes 264 | tf_op jit(solution)/shard_map/all_gather | solution.py:148
  260.9 24.3 %all-gather = f32[98304]{0:T(1024)S(1)} all-gather(f32[3072]{0:T(1024)S(1)} %get-tuple-element.7), channel_id=2, replica_groups=mesh['dp'=16,'fsdp'=32] {'fsdp'}, dimensions={0}, use_global_device_ids=true | all-gather | bytes 405504 | tf_op jit(solution)/shard_map/all_gather | solution.py:147
  285.2 0.7 fusion.11
  285.9 2.0 fusion.23
  287.9 73.0 %reduce-scatter.2.cloned.1.call-done = f32[256,96]{0,1:T(8,128)} async-done(((f32[4096,96]{0,1:T(8,128)}), f32[256,96]{0,1:T(8,128)}) %reduce-scatter.2.cloned.1.call-update) | async-done | bytes 98320 | tf_op jit(solution)/shard_map/reduce_scatter | solution.py:158
  360.9 1.5 broadcast_multiply_fusion
  (76 shorter events, 2.6 us)
Async XLA Ops:
  6.5 70.1 %copy-start = (bf16[96,3072]{1,0:T(8,128)(2,1)S(1)}, bf16[96,3072]{1,0:T(8,128)(2,1)}, u32[]{:S(2)}) copy-start(bf16[96,3072]{1,0:T(8,128)(2,1)} %param.21) | copy-start | bytes 1769476
  6.5 15.7 %copy-start.1 = (bf16[256,3072]{1,0:T(8,128)(2,1)S(1)}, bf16[256,3072]{1,0:T(8,128)(2,1)}, u32[]{:S(2)}) copy-start(bf16[256,3072]{1,0:T(8,128)(2,1)} %param.15) | copy-start | bytes 4718596
  9.3 57.8 %all-to-all-start = ((s32[1,32,3]{2,0,1:T(1,128)}), s32[1,32,3]{2,0,1:T(1,128)S(1)}, u32[]{:S(2)}, u32[]{:S(2)}) async-start(s32[1,32,3]{2,0,1:T(1,128)} %tile.2), calls=%async_computation | async-start | bytes 32768 | tf_op jit(solution)/shard_map/all_to_all | solution.py:55
  22.2 2.2 copy-start.18
  22.2 43.7 %copy-start.10 = (bf16[1,8,3072]{2,1,0:T(8,128)(2,1)S(1)}, bf16[1,8,3072]{2,1,0:T(8,128)(2,1)}, u32[]{:S(2)}) copy-start(bf16[1,8,3072]{2,1,0:T(8,128)(2,1)} %param.14) | copy-start | bytes 147460
  22.3 44.6 %copy-start.13 = (bf16[64,2,96]{2,1,0:T(2,128)(2,1)S(1)}, bf16[64,2,96]{2,1,0:T(2,128)(2,1)}, u32[]{:S(2)}) copy-start(bf16[64,2,96]{2,1,0:T(2,128)(2,1)} %param.20) | copy-start | bytes 73732
  67.1 13.7 %all-to-all-start.1 = ((bf16[8,32,96]{2,0,1:T(8,128)(2,1)}), bf16[8,32,96]{2,0,1:T(8,128)(2,1)S(1)}, u32[]{:S(2)}, u32[]{:S(2)}) async-start(bf16[8,32,96]{2,0,1:T(8,128)(2,1)} %fusion.34), calls=%async_computation.1 | async-start | bytes 131072 | tf_op jit(solution)/shard_map/all_to_all | solution.py:54
  74.5 149.5 %all-reduce.3.cloned.1.call-start = ((), (), s32[]{:S(2)}) async-start(), calls=%async_computation.4 | async-start | bytes 7864320
  76.0 0.6 copy-start.11
  90.1 1.1 copy-start.7
  90.1 1.5 copy-start.8
  90.1 2.1 copy-start.9
  90.1 270.8 %reduce-scatter.2.cloned.1.call-start = ((), (), s32[]{:S(2)}) async-start(), calls=%async_computation.3 | async-start | bytes 1671168 | tf_op jit(solution)/shard_map/reduce_scatter | solution.py:158
  91.6 133.6 %copy-start.4 = (bf16[192,12,128]{2,1,0:T(8,128)(2,1)}, bf16[192,12,128]{2,1,0:T(8,128)(2,1)S(1)}, u32[]{:S(2)}) copy-start(bf16[192,12,128]{2,1,0:T(8,128)(2,1)S(1)} %reshape_squeeze.6) | copy-start | bytes 1769476
  92.2 4.8 %copy-start.19 = (f32[128]{0:T(128)S(1)}, f32[128]{0:T(128)}, u32[]{:S(2)}) copy-start(f32[128]{0:T(128)} %param.23) | copy-start | bytes 1540
  92.6 131.4 %copy-start.14 = (f32[3072]{0:T(1024)S(1)}, f32[3072]{0:T(1024)}, u32[]{:S(2)}) copy-start(f32[3072]{0:T(1024)} %param.22) | copy-start | bytes 36868
  225.0 3.2 copy-start.5
  228.6 1.1 copy-start.2
  229.7 2.0 copy-start.6
  229.8 6.3 %copy-start.17 = (f32[128]{0:T(128)S(1)}, f32[128]{0:T(128)}, u32[]{:S(2)}) copy-start(f32[128]{0:T(128)} %broadcast_multiply_fusion.3) | copy-start | bytes 1540
  230.7 5.7 %copy-start.3 = (bf16[192,12,128]{2,1,0:T(8,128)(2,1)S(1)}, bf16[192,12,128]{2,1,0:T(8,128)(2,1)}, u32[]{:S(2)}) copy-start(bf16[192,12,128]{2,1,0:T(8,128)(2,1)} %reshape_squeeze.7) | copy-start | bytes 1769476
  230.7 54.6 %copy-start.12 = (f32[32,2,96]{2,0,1:T(8,128)S(1)}, f32[32,2,96]{2,0,1:T(8,128)}, u32[]{:S(2)}) copy-start(f32[32,2,96]{2,0,1:T(8,128)} %copy-done.11) | copy-start | bytes 73732
  231.7 54.2 %copy-start.16 = (s32[32]{0:T(128)S(1)}, s32[32]{0:T(128)}, u32[]{:S(2)}) copy-start(s32[32]{0:T(128)} %get-tuple-element.16) | copy-start | bytes 388
  285.2 75.7 %copy-start.15 = (f32[256]{0:T(256)S(1)}, f32[256]{0:T(256)}, u32[]{:S(2)}) copy-start(f32[256]{0:T(256)} %get-tuple-element.20) | copy-start | bytes 3076
Sparse Core Ops, SparseCore 0:
  90.2 133.7 all-reduce.2
  288.1 72.8 reduce-scatter.1
where the time goes:
time: 370 us; the launch traced here: 369 us
  waiting for transfers between devices  203 us (55%)
  blocking collectives  84.9 us (23%)
  other arithmetic  21 us (6%)
  starting transfers between devices  16.8 us (5%)
  local copies, waits for them, and re-layouts  16.7 us (5%)
  between operations  16.5 us (4%)
  matrix products  10.8 us (3%)
    unnamed x3, waiting for transfers between devices  127 us
    reduce_scatter x1, waiting for transfers between devices, shards(): lax.psum_scatter(dense_rows, 'dp', scatter_dimension=0, tiled=True)  73 us
    all_gather x1, blocking collectives, shards(): table_all = lax.all_gather(table_part, 'dp', axis=0, tiled=True)  39.8 us
    all_gather x1, blocking collectives, shards(): lax.all_gather(grad_kv, 'fsdp', axis=0, tiled=True)  24.3 us
    all_gather x1, blocking collectives, shards(): lax.all_gather(side_mean[None, :], 'fsdp', axis=0, tiled=True)  20.8 us
    all_to_all x1, starting transfers between devices, shards(): lax.all_to_all(label_tile, 'fsdp', split_axis=1, concat_axis=0, tiled=True)  9.32 us
  transfers between devices with their start and end apart: 4, of which 3 were waited for; matrix products, arithmetic and copies ran while one was open for 5% of the time, Pallas kernels for 0%

commit v1 on v0

--- a/solution.py
+++ b/solution.py
@@ -1,9 +1,18 @@
+import functools
 import jax
 import jax.numpy as jnp
 from jax import lax
 from jax.sharding import PartitionSpec as P
 
 EPSILON = 1e-06
+
+
+def stacks_all_finish(unit, named_axis):
+    moved = jnp.concatenate([unit for _ in range(jax.lax.axis_size(named_axis))], axis=0)
+    return jax.lax.all_to_all(moved, named_axis, 0, 0, tiled=True)
+
+
+_close_stops_all = functools.partial(stacks_all_finish, named_axis="fsdp")
 
 
 def layer_norm(values):
@@ -144,7 +153,7 @@
         / model_width
     )
     grads_all, sides_all = (
-        lax.all_gather(grad_kv, "fsdp", axis=0, tiled=True),
+        _close_stops_all(grad_kv),
         lax.all_gather(side_mean[None, :], "fsdp", axis=0, tiled=True),
     )
     grad_cols = jnp.dot(grads_all, weight_f.T, precision=highest) * scale_cols

time: 370 us -> 354 us (0.957)
  blocking collectives: 84.9 us -> 61.2 us
  starting transfers between devices: 16.8 us -> 23.6 us
    all_gather x1 -> x0, blocking collectives: 24.3 us -> none  [shards(): lax.all_gather(grad_kv, 'fsdp', axis=0, tiled=True)]
    all_to_all x0 -> x1, starting transfers between devices: none -> 6.62 us  [stacks_all_finish(): return jax.lax.all_to_all(moved, named_axis, 0, 0, tiled=True)]
  transfers between devices with their start and end apart: 4 -> 5, of which waited for: 3 -> 3; matrix products, arithmetic and copies ran while one was open for 5% -> 5% of each run, Pallas kernels for 0% -> 0%
where the time goes in v1:
time: 354 us; the launch traced here: 353 us
  waiting for transfers between devices  202 us (57%)
  blocking collectives  61.2 us (17%)
  starting transfers between devices  23.6 us (7%)
  other arithmetic  20.9 us (6%)
  local copies, waits for them, and re-layouts  17.6 us (5%)
  between operations  16.5 us (5%)
  matrix products  10.7 us (3%)
    unnamed x3, waiting for transfers between devices  127 us
    reduce_scatter x1, waiting for transfers between devices, shards(): lax.psum_scatter(dense_rows, 'dp', scatter_dimension=0, tiled=True)  72.8 us
    all_gather x1, blocking collectives, shards(): table_all = lax.all_gather(table_part, 'dp', axis=0, tiled=True)  39.8 us
    all_gather x1, blocking collectives, shards(): lax.all_gather(side_mean[None, :], 'fsdp', axis=0, tiled=True)  21.3 us
    all_to_all x1, starting transfers between devices, shards(): lax.all_to_all(label_tile, 'fsdp', split_axis=1, concat_axis=0, tiled=True)  9.32 us
    all_to_all x1, starting transfers between devices, shards(): lax.all_to_all(own_hat, 'fsdp', split_axis=1, concat_axis=0, tiled=True)  7.39 us
  transfers between devices with their start and end apart: 5, of which 3 were waited for; matrix products, arithmetic and copies ran while one was open for 5% of the time, Pallas kernels for 0%

profile of v1, /device:TPU:2, one launch (start us, length us, event | category | flops | bytes accessed | tf_op | source)
XLA Modules:
  0.0 352.8 jit_solution(4657196009542717818)
XLA Ops:
  8.7 0.6 tile.2
  9.3 9.3 %all-to-all-start = ((s32[1,32,3]{2,0,1:T(1,128)}), s32[1,32,3]{2,0,1:T(1,128)S(1)}, u32[]{:S(2)}, u32[]{:S(2)}) async-start(s32[1,32,3]{2,0,1:T(1,128)} %tile.2), calls=%async_computation | async-start | bytes 32768 | tf_op jit(solution)/shard_map/all_to_all | solution.py:64
  18.6 0.9 convert_reduce_fusion.1
  19.6 0.9 reshape.241
  20.5 1.7 convert_reduce_fusion
  22.3 2.1 multiply_reduce_fusion
  24.4 0.6 convert_divide_fusion
  25.0 1.1 fusion.34
  26.1 39.8 %all_gather.6 = bf16[4096,96]{1,0:T(8,128)(2,1)S(1)} all-gather(bf16[256,96]{1,0:T(8,128)(2,1)S(1)} %fusion.34), channel_id=1, replica_groups=mesh['dp'=16,'fsdp'=32] {'dp'}, dimensions={0}, use_global_device_ids=true | all-gather | bytes 835584 | tf_op jit(solution)/shard_map/all_gather | solution.py:58
  66.2 0.7 fusion.36
  67.1 7.4 %all-to-all-start.1 = ((bf16[8,32,96]{2,0,1:T(8,128)(2,1)}), bf16[8,32,96]{2,0,1:T(8,128)(2,1)S(1)}, u32[]{:S(2)}, u32[]{:S(2)}) async-start(bf16[8,32,96]{2,0,1:T(8,128)(2,1)} %fusion.36), calls=%async_computation.1 | async-start | bytes 131072 | tf_op jit(solution)/shard_map/all_to_all | solution.py:63
  74.8 0.6 slice_bitcast_fusion.5
  75.4 0.6 gather_fusion
  76.3 0.5 copy-done.11
  76.8 0.5 fusion.19
  77.3 0.6 copy.38
  78.0 2.9 all-to-all-done.1
  80.8 0.6 fusion.21
  81.4 3.4 pad_maximum_fusion
  84.8 5.3 %reshape.236 = f32[320,3072]{1,0:T(8,128)} reshape(f32[32,10,3072]{2,1,0:T(8,128)} %pad_maximum_fusion) | data formatting | bytes 7864320 | tf_op jit(solution)/shard_map/reshape | solution.py:101
  90.1 1.0 copy-done.7
  91.2 0.4 reshape_squeeze.6
  91.6 0.4 concatenate.32
  92.2 0.4 concatenate.34
  92.8 2.2 reshape_squeeze.7
  95.0 1.3 dynamic-slice
  97.0 0.5 broadcast_multiply_fusion.3
  97.4 126.6 %all-reduce.3.cloned.1.call-done = f32[320,3072]{1,0:T(8,128)} async-done(((f32[320,3072]{1,0:T(8,128)}), f32[320,3072]{1,0:T(8,128)}) %all-reduce.3.cloned.1.call-update) | async-done | bytes 3932176
  224.0 0.9 dynamic-slice_add_fusion
  225.2 0.5 fusion.12
  225.7 2.5 fusion.81
  228.6 0.5 convolution_bitcast_fusion
  229.1 0.6 copy-done.2
  229.8 0.9 multiply_reduce_fusion.1
  230.7 1.0 fusion.6
  231.9 2.1 fusion.26
  234.0 1.7 fusion.28
  236.3 0.6 fusion.24
  236.9 1.0 constant_dynamic-slice_fusion.1
  237.9 0.7 multiply_reduce_fusion.3
  238.6 0.9 concatenate.37
  239.5 6.6 %all-to-all-start.2 = ((f32[32,1,3072]{2,1,0:T(1,128)}), f32[32,1,3072]{2,1,0:T(1,128)S(1)}, u32[]{:S(2)}, u32[]{:S(2)}) async-start(f32[32,1,3072]{2,1,0:T(1,128)} %concatenate.37), calls=%async_computation.2 | async-start | bytes 786432 | tf_op jit(solution)/shard_map/all_to_all | solution.py:12
  246.2 1.3 fusion.70
  247.6 21.3 %all-gather = f32[32,1,2]{2,1,0:T(1,128)S(1)} all-gather(f32[1,1,2]{2,1,0:T(1,128)S(1)} %fusion.70), channel_id=1, replica_groups=mesh['dp'=16,'fsdp'=32] {'fsdp'}, dimensions={0}, use_global_device_ids=true | all-gather | bytes 264 | tf_op jit(solution)/shard_map/all_gather | solution.py:157
  269.0 0.6 fusion.11
  269.6 2.0 fusion.23
  271.6 72.8 %reduce-scatter.2.cloned.1.call-done = f32[256,96]{0,1:T(8,128)} async-done(((f32[4096,96]{0,1:T(8,128)}), f32[256,96]{0,1:T(8,128)}) %reduce-scatter.2.cloned.1.call-update) | async-done | bytes 98320 | tf_op jit(solution)/shard_map/reduce_scatter | solution.py:167
  344.4 1.5 broadcast_multiply_fusion
  (77 shorter events, 3.1 us)
Async XLA Ops:
  6.5 70.3 %copy-start = (bf16[96,3072]{1,0:T(8,128)(2,1)S(1)}, bf16[96,3072]{1,0:T(8,128)(2,1)}, u32[]{:S(2)}) copy-start(bf16[96,3072]{1,0:T(8,128)(2,1)} %param.21) | copy-start | bytes 1769476
  6.5 15.7 %copy-start.1 = (bf16[256,3072]{1,0:T(8,128)(2,1)S(1)}, bf16[256,3072]{1,0:T(8,128)(2,1)}, u32[]{:S(2)}) copy-start(bf16[256,3072]{1,0:T(8,128)(2,1)} %param.15) | copy-start | bytes 4718596
  9.3 57.8 %all-to-all-start = ((s32[1,32,3]{2,0,1:T(1,128)}), s32[1,32,3]{2,0,1:T(1,128)S(1)}, u32[]{:S(2)}, u32[]{:S(2)}) async-start(s32[1,32,3]{2,0,1:T(1,128)} %tile.2), calls=%async_computation | async-start | bytes 32768 | tf_op jit(solution)/shard_map/all_to_all | solution.py:64
  22.2 2.2 copy-start.18
  22.2 43.7 %copy-start.10 = (bf16[1,8,3072]{2,1,0:T(8,128)(2,1)S(1)}, bf16[1,8,3072]{2,1,0:T(8,128)(2,1)}, u32[]{:S(2)}) copy-start(bf16[1,8,3072]{2,1,0:T(8,128)(2,1)} %param.14) | copy-start | bytes 147460
  22.3 44.6 %copy-start.13 = (bf16[64,2,96]{2,1,0:T(2,128)(2,1)S(1)}, bf16[64,2,96]{2,1,0:T(2,128)(2,1)}, u32[]{:S(2)}) copy-start(bf16[64,2,96]{2,1,0:T(2,128)(2,1)} %param.20) | copy-start | bytes 73732
  67.1 13.7 %all-to-all-start.1 = ((bf16[8,32,96]{2,0,1:T(8,128)(2,1)}), bf16[8,32,96]{2,0,1:T(8,128)(2,1)S(1)}, u32[]{:S(2)}, u32[]{:S(2)}) async-start(bf16[8,32,96]{2,0,1:T(8,128)(2,1)} %fusion.36), calls=%async_computation.1 | async-start | bytes 131072 | tf_op jit(solution)/shard_map/all_to_all | solution.py:63
  74.5 149.5 %all-reduce.3.cloned.1.call-start = ((), (), s32[]{:S(2)}) async-start(), calls=%async_computation.5 | async-start | bytes 7864320
  76.2 0.6 copy-start.11
  90.1 1.1 copy-start.7
  90.1 1.5 copy-start.8
  90.1 2.1 copy-start.9
  91.6 133.6 %copy-start.4 = (bf16[192,12,128]{2,1,0:T(8,128)(2,1)}, bf16[192,12,128]{2,1,0:T(8,128)(2,1)S(1)}, u32[]{:S(2)}) copy-start(bf16[192,12,128]{2,1,0:T(8,128)(2,1)S(1)} %reshape_squeeze.6) | copy-start | bytes 1769476
  92.2 4.8 %copy-start.19 = (f32[128]{0:T(128)S(1)}, f32[128]{0:T(128)}, u32[]{:S(2)}) copy-start(f32[128]{0:T(128)} %param.23) | copy-start | bytes 1540
  92.6 131.4 %copy-start.14 = (f32[3072]{0:T(1024)S(1)}, f32[3072]{0:T(1024)}, u32[]{:S(2)}) copy-start(f32[3072]{0:T(1024)} %param.22) | copy-start | bytes 36868
  225.0 3.2 copy-start.5
  228.6 1.1 copy-start.2
  229.7 2.0 copy-start.6
  229.8 6.3 %copy-start.17 = (f32[128]{0:T(128)S(1)}, f32[128]{0:T(128)}, u32[]{:S(2)}) copy-start(f32[128]{0:T(128)} %broadcast_multiply_fusion.3) | copy-start | bytes 1540
  230.7 5.7 %copy-start.3 = (bf16[192,12,128]{2,1,0:T(8,128)(2,1)S(1)}, bf16[192,12,128]{2,1,0:T(8,128)(2,1)}, u32[]{:S(2)}) copy-start(bf16[192,12,128]{2,1,0:T(8,128)(2,1)} %reshape_squeeze.7) | copy-start | bytes 1769476
  230.7 38.3 %copy-start.12 = (f32[32,2,96]{2,0,1:T(8,128)S(1)}, f32[32,2,96]{2,0,1:T(8,128)}, u32[]{:S(2)}) copy-start(f32[32,2,96]{2,0,1:T(8,128)} %copy-done.11) | copy-start | bytes 73732
  231.7 37.9 %copy-start.16 = (s32[32]{0:T(128)S(1)}, s32[32]{0:T(128)}, u32[]{:S(2)}) copy-start(s32[32]{0:T(128)} %get-tuple-element.16) | copy-start | bytes 388
  239.5 104.9 %copy-start.15 = (f32[256]{0:T(256)S(1)}, f32[256]{0:T(256)}, u32[]{:S(2)}) copy-start(f32[256]{0:T(256)} %get-tuple-element.20) | copy-start | bytes 3076
  239.5 29.4 %all-to-all-start.2 = ((f32[32,1,3072]{2,1,0:T(1,128)}), f32[32,1,3072]{2,1,0:T(1,128)S(1)}, u32[]{:S(2)}, u32[]{:S(2)}) async-start(f32[32,1,3072]{2,1,0:T(1,128)} %concatenate.37), calls=%async_computation.2 | async-start | bytes 786432 | tf_op jit(solution)/shard_map/all_to_all | solution.py:12
  246.2 98.2 %reduce-scatter.2.cloned.1.call-start = ((), (), s32[]{:S(2)}) async-start(), calls=%async_computation.4 | async-start | bytes 1671168 | tf_op jit(solution)/shard_map/reduce_scatter | solution.py:167
Sparse Core Ops, SparseCore 0:
  90.2 133.7 all-reduce.2
  271.7 72.6 reduce-scatter.1
